TPU v7x, 512 devices: a whole 4x8x8 slice. The times are simulated.
512 devices in a mesh: row: 16 (over z, y_hi), col: 32 (over x, y_lo, core).
Axes of the slice: x: 4, y: 8 (y_hi: 2, y_lo: 4; y = y_hi * 4 + y_lo), z: 8, core: 2. Of those that a mesh axis runs over, the one named last changes fastest.
Arguments:
- scalars: float32 [1, 256, 256, 512], P(None, 'row', 'col'), may hold values from -6 to 6
- velocity: bfloat16 [3, 256, 256, 512], P(None, 'row', 'col'), may hold values from -6 to 6
- first_x: bfloat16 [512, 512], replicated, may hold values from -0.25 to 0.25
- second_x: bfloat16 [512, 512], replicated, may hold values from -0.25 to 0.25
- first_y: bfloat16 [256, 256], replicated, may hold values from -0.375 to 0.375
- second_y: bfloat16 [256, 256], replicated, may hold values from -0.375 to 0.375
- first_z: bfloat16 [256, 256], replicated, may hold values from -0.375 to 0.375
- second_z: bfloat16 [256, 256], replicated, may hold values from -0.375 to 0.375
Outputs:
- updated: float32 [1, 256, 256, 512], P(None, 'row', 'col')
All inputs are finite; a program needn't handle non-finite values.
Results may differ from a plain program's by a relative error of at most 0.0021.
Values may be sent and summed in bfloat16 or wider, within the bound.
No kernel may reach another device: no remote copies, remote signals or barrier semaphores. Data moves between devices by JAX's collectives and lax.ppermute only.
A program may use at most 64 MiB of HBM per device.

v0:
```python
import jax
import jax.numpy as jnp
from jax import lax
from jax.sharding import PartitionSpec as P

diffusion_coefficient = 0.5
step_weight = 0.5


def contract_last(scalar_values, matrix):
    return lax.dot_general(
        scalar_values,
        matrix,
        (((scalar_values.ndim - 1,), (1,)), ((), ())),
        preferred_element_type=jnp.float32,
    )


def contract_middle(scalar_values, matrix):
    return jnp.einsum("syc,ky->skc", scalar_values, matrix, preferred_element_type=jnp.float32)


def contract_z(scalar_values, matrix):
    blocks = scalar_values.shape[2]
    depth_z = scalar_values.shape[4]
    shaped = matrix.reshape(matrix.shape[0] // depth_z, depth_z, blocks, depth_z)
    return jnp.einsum(
        "sajxz,JZjz->saJxZ", scalar_values, shaped, preferred_element_type=jnp.float32
    )


def derivative_pair(scalar_values, first_derivative_matrix, second_derivative_matrix, apply_matrix):
    return (
        apply_matrix(scalar_values, first_derivative_matrix),
        apply_matrix(scalar_values, second_derivative_matrix),
    )


def axis_contribution(
    scalar_values, velocity_field, first_derivative_matrix, second_derivative_matrix, apply_matrix
):
    velocity_flux = velocity_field.astype(jnp.float32)
    flux_product = (velocity_flux * scalar_values.astype(jnp.float32)).astype(jnp.bfloat16)
    scalar_gradient, second_derivative = derivative_pair(
        scalar_values, first_derivative_matrix, second_derivative_matrix, apply_matrix
    )
    advected_scalar = apply_matrix(flux_product, first_derivative_matrix)
    return (
        -0.5 * (velocity_flux * scalar_gradient + advected_scalar)
        + diffusion_coefficient * second_derivative
    )


def body(scalars, velocity, first_x, second_x, first_y, second_y, first_z, second_z):
    scalar_count = scalars.shape[0]
    rows_local = scalars.shape[1]
    depth_z = scalars.shape[2]
    length_x = scalars.shape[3]
    compiled_step = scalars.astype(jnp.bfloat16)
    x_term = axis_contribution(compiled_step, velocity[0], first_x, second_x, contract_last)
    outgoing = jnp.concatenate([compiled_step, velocity[1:]], axis=0)
    outgoing = jnp.transpose(outgoing, (0, 1, 3, 2)).reshape(
        scalar_count + 2, rows_local, length_x * depth_z
    )
    pencil_y = lax.all_to_all(outgoing, "row", split_axis=2, concat_axis=1, tiled=True)
    y_term = axis_contribution(
        pencil_y[:scalar_count], pencil_y[scalar_count], first_y, second_y, contract_middle
    )
    onward = jnp.concatenate([pencil_y[:scalar_count], pencil_y[scalar_count + 1 :]], axis=0)
    pencil_z = lax.all_to_all(onward, "col", split_axis=1, concat_axis=2, tiled=True)
    blocks = lax.axis_size("col")
    width_y = pencil_z.shape[1]
    columns = pencil_y.shape[2]
    pencil_z = pencil_z.reshape(scalar_count + 1, width_y, blocks, columns // depth_z, depth_z)
    z_term = axis_contribution(
        pencil_z[:scalar_count], pencil_z[scalar_count], first_z, second_z, contract_z
    )
    z_term = z_term.reshape(scalar_count, width_y, blocks * columns)
    z_lines = lax.all_to_all(z_term, "col", split_axis=2, concat_axis=1, tiled=True)
    y_back_part, z_back_part = (
        lax.all_to_all(y_term, "row", split_axis=1, concat_axis=2, tiled=True),
        lax.all_to_all(z_lines, "row", split_axis=1, concat_axis=2, tiled=True),
    )
    returned = y_back_part + z_back_part
    returned = returned.reshape(scalar_count, rows_local, length_x, depth_z)
    returned = jnp.transpose(returned, (0, 1, 3, 2))
    return scalars + step_weight * (x_term + returned)


def solution(mesh):
    return jax.shard_map(
        body,
        mesh=mesh,
        in_specs=(
            P(None, "row", "col", None),
            P(None, "row", "col", None),
            P(),
            P(),
            P(),
            P(),
            P(),
            P(),
        ),
        out_specs=P(None, "row", "col", None),
        check_vma=False,
    )
```

profile of v0, /device:TPU:8, one launch (start us, length us, event | category | flops | bytes accessed | tf_op | source)
XLA Modules:
  0.0 201.4 jit_solution(11211925408046868918)
XLA Ops:
  0.0 0.0 copy-start
  0.0 1.0 convert_element_type.74
  1.0 1.0 slice.32
  2.1 3.4 %copy.35 = bf16[3,16,512,8]{1,3,2,0:T(8,128)(2,1)} copy(bf16[3,16,512,8]{2,3,1,0:T(8,128)(2,1)S(1)} %maximum_bitcast_fusion) | data formatting | bytes 786432 | tf_op jit(solution)/shard_map/transpose | solution.py:62
  5.5 6.8 %copy.95 = bf16[3,16,4096]{1,0,2:T(4,128)(2,1)} copy(bf16[3,16,4096]{1,2,0:T(8,128)(2,1)} %bitcast.143) | data formatting | bytes 786432 | tf_op jit(solution)/shard_map/reshape | solution.py:62
  12.3 6.6 %reshape.147 = bf16[16,2,6144]{2,1,0:T(2,128)(2,1)S(1)} reshape(bf16[4096,3,16]{2,1,0:T(4,128)(2,1)} %bitcast.140) | data formatting | bytes 786432
  18.9 33.6 %all_to_all.66 = bf16[16,2,6144]{2,1,0:T(2,128)(2,1)S(1)} all-to-all(bf16[16,2,6144]{2,1,0:T(2,128)(2,1)S(1)} %reshape.147), channel_id=1, replica_groups=mesh['row'=16,'col'=32] {'row'}, dimensions={0} | all-to-all | bytes 786432 | tf_op jit(solution)/shard_map/all_to_all | solution.py:65
  52.5 5.6 %reshape.148 = bf16[4096,3,16]{2,1,0:T(4,128)(2,1)} reshape(bf16[16,2,6144]{2,1,0:T(2,128)(2,1)S(1)} %all_to_all.66) | data formatting | bytes 786432
  58.1 0.0 copy-start.6
  58.1 4.2 %copy.71 = bf16[3,16,16,256]{3,2,1,0:T(8,128)(2,1)S(1)} copy(bf16[3,16,16,256]{1,0,3,2:T(4,128)(2,1)} %bitcast.141) | data formatting | bytes 786432 | tf_op jit(solution)/shard_map/all_to_all | solution.py:65
  62.5 1.0 copy.44
  63.5 5.9 %all-to-all-start.2 = ((bf16[2,256,256]{2,0,1:T(2,128)(2,1)}), bf16[2,256,256]{2,0,1:T(2,128)(2,1)S(1)}, u32[]{:S(2)}, u32[]{:S(2)}) async-start(bf16[2,256,256]{2,0,1:T(2,128)(2,1)} %copy.44), calls=%async_computation.2 | async-start | bytes 524288 | tf_op jit(solution)/shard_map/all_to_all | solution.py:70
  69.4 0.0 copy-done.6
  69.4 2.5 %reshape.130 = bf16[32,8,32,8]{3,2,1,0:T(8,128)(2,1)S(1)} reshape(bf16[256,256]{1,0:T(8,128)(2,1)S(1)} %copy-done.6) | data formatting | bytes 262144 | tf_op jit(solution)/shard_map/reshape | solution.py:26
  71.9 1.9 copy.49
  73.8 3.4 %reshape.131 = bf16[32,8,32,8]{3,2,1,0:T(8,128)(2,1)S(1)} reshape(bf16[256,256]{1,0:T(8,128)(2,1)} %param.15) | data formatting | bytes 262144 | tf_op jit(solution)/shard_map/reshape | solution.py:26
  77.2 1.9 copy.55
  79.0 0.2 copy.38
  79.2 0.1 copy.40
  79.3 0.0 all-to-all-done.2
  79.5 1.0 copy.47
  80.5 0.0 copy-start.3
  80.5 0.4 copy.46
  80.9 1.0 copy.51
  81.9 0.0 copy-start.4
  81.9 2.0 fusion.1
  83.9 2.0 fusion.5
  85.9 0.0 copy-done.3
  85.9 0.0 copy-done.4
  85.9 0.7 fusion.4
  86.6 4.3 %copy.78 = f32[1,8,32,32,8]{1,4,3,2,0:T(8,128)} copy(f32[1,8,32,32,8]{2,3,4,1,0:T(8,128)S(1)} %fusion.4) | data formatting | bytes 524288 | tf_op jit(solution)/shard_map/reshape | solution.py:78
  91.0 0.6 broadcast.21
  91.5 38.4 %reduce = f32[8192,8]{1,0:T(8,128)} reduce(f32[8192,1,8]{2,1,0:T(1,128)} %bitcast.139, f32[]{:T(128)} %broadcast.21), dimensions={1}, to_apply=%bitcast.128.reduce_sub_computation | reduce | bytes 524292
  130.0 0.0 copy-start.5
  130.0 0.0 copy-start.7
  130.0 4.5 %reshape.149 = f32[32,1,2048]{2,1,0:T(1,128)} reshape(f32[8192,8]{1,0:T(8,128)} %reduce) | data formatting | bytes 524288
  134.5 7.7 %all-to-all-start.3 = ((f32[32,1,2048]{2,1,0:T(1,128)}), f32[32,1,2048]{2,1,0:T(1,128)S(1)}, u32[]{:S(2)}, u32[]{:S(2)}) async-start(f32[32,1,2048]{2,1,0:T(1,128)} %reshape.149), calls=%async_computation.3 | async-start | bytes 524288 | tf_op jit(solution)/shard_map/all_to_all | solution.py:79
  142.2 0.0 copy-done.5
  142.2 0.2 fusion.14
  142.5 0.2 fusion.13
  142.7 0.0 copy-done.7
  142.7 0.2 fusion.8
  142.9 0.8 copy.41
  143.8 7.7 %all-to-all-done.3 = f32[32,1,2048]{2,1,0:T(1,128)S(1)} async-done(((f32[32,1,2048]{2,1,0:T(1,128)}), f32[32,1,2048]{2,1,0:T(1,128)S(1)}, u32[]{:S(2)}, u32[]{:S(2)}) %all-to-all-start.3) | async-done | bytes 262176 | tf_op jit(solution)/shard_map/all_to_all | solution.py:79
  151.5 4.2 %all-to-all-start.1 = ((f32[1,256,256]{2,0,1:T(1,128)}), f32[1,256,256]{2,0,1:T(1,128)S(1)}, u32[]{:S(2)}, u32[]{:S(2)}) async-start(f32[1,256,256]{2,0,1:T(1,128)} %copy.41), calls=%async_computation.1 | async-start | bytes 524288 | tf_op jit(solution)/shard_map/all_to_all | solution.py:81
  155.7 1.3 reduce.1
  157.0 0.0 copy-start.2
  157.0 8.4 %reshape.150 = f32[8192,1,8]{2,1,0:T(1,128)} reshape(f32[32,2048]{1,0:T(8,128)S(1)} %reduce.1) | data formatting | bytes 524288
  165.4 2.8 %copy.79 = f32[1,8,32,256]{3,2,1,0:T(8,128)S(1)} copy(f32[1,8,32,256]{1,3,2,0:T(8,128)} %bitcast.142) | data formatting | bytes 524288 | tf_op jit(solution)/shard_map/all_to_all | solution.py:79
  168.2 0.2 copy.93
  168.4 1.0 copy.60
  169.4 0.0 copy-start.1
  169.4 2.9 %all-to-all-done.1 = f32[1,256,256]{2,0,1:T(1,128)S(1)} async-done(((f32[1,256,256]{2,0,1:T(1,128)}), f32[1,256,256]{2,0,1:T(1,128)S(1)}, u32[]{:S(2)}, u32[]{:S(2)}) %all-to-all-start.1) | async-done | bytes 262176 | tf_op jit(solution)/shard_map/all_to_all | solution.py:81
  172.3 9.2 %all-to-all-start.4 = ((f32[1,256,256]{2,0,1:T(1,128)}), f32[1,256,256]{2,0,1:T(1,128)S(1)}, u32[]{:S(2)}, u32[]{:S(2)}) async-start(f32[1,256,256]{2,0,1:T(1,128)} %copy.60), calls=%async_computation.4 | async-start | bytes 524288 | tf_op jit(solution)/shard_map/all_to_all | solution.py:82
  181.5 0.0 copy-done
  181.5 0.0 copy-done.2
  181.5 0.3 convolution_multiply_fusion.2
  181.9 0.3 fusion.9
  182.2 15.7 %all-to-all-done.4 = f32[1,256,256]{2,0,1:T(1,128)S(1)} async-done(((f32[1,256,256]{2,0,1:T(1,128)}), f32[1,256,256]{2,0,1:T(1,128)S(1)}, u32[]{:S(2)}, u32[]{:S(2)}) %all-to-all-start.4) | async-done | bytes 262176 | tf_op jit(solution)/shard_map/all_to_all | solution.py:82
  197.9 0.6 copy.63
  198.5 0.8 copy.64
  199.3 0.0 copy-done.1
  199.3 2.1 %fusion.17 = f32[1,16,8,512]{3,2,1,0:T(8,128)} fusion(f32[1,16,8,512]{3,2,1,0:T(8,128)S(1)} %copy-done.1, f32[16,8,512]{2,1,0:T(8,128)S(1)} %fusion.9, bf16[512,512]{1,0:T(8,128)(2,1)} %param.11, f32[1,16,512,8]{2,3,1,0:T(8,128)S(1)} %copy.64, bf16[1,16,8,512]{3,2,1,0:T(8,128)(2,1)S(1)} %convert_element_type.74), kind=kOutput, calls=%fused_computation.26 | convolution fusion | flops 67436544 | bytes 1703936 | tf_op jit(solution)/shard_map/dot_general | solution.py:11
  (9 shorter events, 0.3 us)
Async XLA Ops:
  0.0 181.5 %copy-start = (bf16[512,512]{1,0:T(8,128)(2,1)S(1)}, bf16[512,512]{1,0:T(8,128)(2,1)}, u32[]{:S(2)}) copy-start(bf16[512,512]{1,0:T(8,128)(2,1)} %param.10) | copy-start | bytes 1572868
  58.1 11.3 %copy-start.6 = (bf16[256,256]{1,0:T(8,128)(2,1)S(1)}, bf16[256,256]{1,0:T(8,128)(2,1)}, u32[]{:S(2)}) copy-start(bf16[256,256]{1,0:T(8,128)(2,1)} %param.14) | copy-start | bytes 393220
  63.5 15.9 %all-to-all-start.2 = ((bf16[2,256,256]{2,0,1:T(2,128)(2,1)}), bf16[2,256,256]{2,0,1:T(2,128)(2,1)S(1)}, u32[]{:S(2)}, u32[]{:S(2)}) async-start(bf16[2,256,256]{2,0,1:T(2,128)(2,1)} %copy.44), calls=%async_computation.2 | async-start | bytes 524288 | tf_op jit(solution)/shard_map/all_to_all | solution.py:70
  80.5 5.4 %copy-start.3 = (bf16[32,8,32,8]{2,0,3,1:T(8,128)(2,1)S(1)}, bf16[32,8,32,8]{2,0,3,1:T(8,128)(2,1)}, u32[]{:S(2)}) copy-start(bf16[32,8,32,8]{2,0,3,1:T(8,128)(2,1)} %copy.49) | copy-start | bytes 393220
  81.9 4.0 %copy-start.4 = (bf16[1,8,32,256]{2,3,1,0:T(8,128)(2,1)S(1)}, bf16[1,8,32,256]{2,3,1,0:T(8,128)(2,1)}, u32[]{:S(2)}) copy-start(bf16[1,8,32,256]{2,3,1,0:T(8,128)(2,1)} %copy.51) | copy-start | bytes 393220
  130.0 12.2 %copy-start.5 = (bf16[256,256]{1,0:T(8,128)(2,1)S(1)}, bf16[256,256]{1,0:T(8,128)(2,1)}, u32[]{:S(2)}) copy-start(bf16[256,256]{1,0:T(8,128)(2,1)} %param.12) | copy-start | bytes 393220
  130.0 12.7 %copy-start.7 = (bf16[256,256]{1,0:T(8,128)(2,1)S(1)}, bf16[256,256]{1,0:T(8,128)(2,1)}, u32[]{:S(2)}) copy-start(bf16[256,256]{1,0:T(8,128)(2,1)} %param.13) | copy-start | bytes 393220
  134.5 17.0 %all-to-all-start.3 = ((f32[32,1,2048]{2,1,0:T(1,128)}), f32[32,1,2048]{2,1,0:T(1,128)S(1)}, u32[]{:S(2)}, u32[]{:S(2)}) async-start(f32[32,1,2048]{2,1,0:T(1,128)} %reshape.149), calls=%async_computation.3 | async-start | bytes 524288 | tf_op jit(solution)/shard_map/all_to_all | solution.py:79
  151.5 20.8 %all-to-all-start.1 = ((f32[1,256,256]{2,0,1:T(1,128)}), f32[1,256,256]{2,0,1:T(1,128)S(1)}, u32[]{:S(2)}, u32[]{:S(2)}) async-start(f32[1,256,256]{2,0,1:T(1,128)} %copy.41), calls=%async_computation.1 | async-start | bytes 524288 | tf_op jit(solution)/shard_map/all_to_all | solution.py:81
  157.0 24.5 %copy-start.2 = (bf16[3,16,8,512]{3,2,1,0:T(8,128)(2,1)S(1)}, bf16[3,16,8,512]{3,2,1,0:T(8,128)(2,1)}, u32[]{:S(2)}) copy-start(bf16[3,16,8,512]{3,2,1,0:T(8,128)(2,1)} %param.9) | copy-start | bytes 1179652
  169.4 30.0 %copy-start.1 = (f32[1,16,8,512]{3,2,1,0:T(8,128)S(1)}, f32[1,16,8,512]{3,2,1,0:T(8,128)}, u32[]{:S(2)}) copy-start(f32[1,16,8,512]{3,2,1,0:T(8,128)} %param.8) | copy-start | bytes 786436
  172.3 25.6 %all-to-all-start.4 = ((f32[1,256,256]{2,0,1:T(1,128)}), f32[1,256,256]{2,0,1:T(1,128)S(1)}, u32[]{:S(2)}, u32[]{:S(2)}) async-start(f32[1,256,256]{2,0,1:T(1,128)} %copy.60), calls=%async_computation.4 | async-start | bytes 524288 | tf_op jit(solution)/shard_map/all_to_all | solution.py:82
where the time goes:
time: 202 us; the launch traced here: 201 us
  local copies, waits for them, and re-layouts  65 us (32%)
  other arithmetic  41 us (20%)
  blocking collectives  33.6 us (17%)
  starting transfers between devices  27 us (13%)
  waiting for transfers between devices  26.4 us (13%)
  matrix products  8.05 us (4%)
    unnamed x1, other arithmetic  38.4 us
    all_to_all x1, blocking collectives, body(): lax.all_to_all(outgoing, 'row', split_axis=2, concat_axis=1, tiled=True)  33.6 us
    unnamed x21, local copies, waits for them, and re-layouts  25.8 us
    all_to_all x1, waiting for transfers between devices, body(): lax.all_to_all(z_lines, 'row', split_axis=1, concat_axis=2, tiled=True)  15.7 us
    reshape x4, local copies, waits for them, and re-layouts, contract_z(): matrix.reshape(matrix.shape[0] // depth_z, depth_z, blocks, depth_z)  9.6 us
    all_to_all x1, starting transfers between devices, body(): lax.all_to_all(z_lines, 'row', split_axis=1, concat_axis=2, tiled=True)  9.23 us
    all_to_all x1, waiting for transfers between devices, body(): lax.all_to_all(z_term, 'col', split_axis=2, concat_axis=1, tiled=True)  7.71 us
    all_to_all x1, starting transfers between devices, body(): lax.all_to_all(z_term, 'col', split_axis=2, concat_axis=1, tiled=True)  7.68 us
  transfers between devices with their start and end apart: 4, of which 3 were waited for; matrix products, arithmetic and copies ran while one was open for 13% of the time, Pallas kernels for 0%

commit v1 on v0

--- a/solution.py
+++ b/solution.py
@@ -62,7 +62,10 @@
     outgoing = jnp.transpose(outgoing, (0, 1, 3, 2)).reshape(
         scalar_count + 2, rows_local, length_x * depth_z
     )
-    pencil_y = lax.all_to_all(outgoing, "row", split_axis=2, concat_axis=1, tiled=True)
+    pencil_y = jnp.concatenate(
+        lax.all_to_all(jnp.stack(jnp.split(outgoing, lax.axis_size("row"), axis=2)), "row", 0, 0),
+        axis=1,
+    )
     y_term = axis_contribution(
         pencil_y[:scalar_count], pencil_y[scalar_count], first_y, second_y, contract_middle
     )

time: 202 us -> 194 us (0.960)
  local copies, waits for them, and re-layouts: 65 us -> 58.5 us
    reshape x1 -> x0, local copies, waits for them, and re-layouts: 6.77 us -> none  [body(): jnp.transpose(outgoing, (0, 1, 3, 2))]
    another operation x0 -> x16, local copies, waits for them, and re-layouts: none -> 4.8 us  [body(): jnp.stack(jnp.split(outgoing, lax.axis_size('row'), axis=2))]
    all_to_all x1, local copies, waits for them, and re-layouts: 4.22 us -> 0.03 us  [body(): lax.all_to_all(jnp.stack(jnp.split(outgoing, lax.axis_size('row'), axis=2...]
    split x0 -> x2, local copies, waits for them, and re-layouts: none -> 3.05 us  [body(): jnp.split(outgoing, lax.axis_size('row'), axis=2)]
    unnamed x21 -> x38, local copies, waits for them, and re-layouts: 25.8 us -> 23.3 us
  transfers between devices with their start and end apart: 4 -> 4, of which waited for: 3 -> 4; matrix products, arithmetic and copies ran while one was open for 13% -> 13% of each run, Pallas kernels for 0% -> 0%
where the time goes in v1:
time: 194 us
  local copies, waits for them, and re-layouts  58.5 us (30%)
  other arithmetic  40.8 us (21%)
  blocking collectives  33.8 us (17%)
  waiting for transfers between devices  26.7 us (14%)
  starting transfers between devices  26.5 us (14%)
  matrix products  6.88 us (4%)
    unnamed x1, other arithmetic  38.4 us
    all_to_all x1, blocking collectives, body(): lax.all_to_all(jnp.stack(jnp.split(outgoing, lax.axis_size('row'), axis=2...  33.8 us
    unnamed x38, local copies, waits for them, and re-layouts  23.3 us
    all_to_all x1, waiting for transfers between devices, body(): lax.all_to_all(z_lines, 'row', split_axis=1, concat_axis=2, tiled=True)  15.7 us
    all_to_all x1, starting transfers between devices, body(): lax.all_to_all(z_lines, 'row', split_axis=1, concat_axis=2, tiled=True)  9.07 us
    reshape x4, local copies, waits for them, and re-layouts, contract_z(): matrix.reshape(matrix.shape[0] // depth_z, depth_z, blocks, depth_z)  8.7 us
    all_to_all x1, waiting for transfers between devices, body(): lax.all_to_all(z_term, 'col', split_axis=2, concat_axis=1, tiled=True)  7.71 us
    all_to_all x1, starting transfers between devices, body(): lax.all_to_all(z_term, 'col', split_axis=2, concat_axis=1, tiled=True)  7.34 us
  transfers between devices with their start and end apart: 4, of which 4 were waited for; matrix products, arithmetic and copies ran while one was open for 13% of the time, Pallas kernels for 0%

profile of v1, /device:TPU:8, one launch (start us, length us, event | category | flops | bytes accessed | tf_op | source)
XLA Modules:
  0.0 193.6 jit_solution(3957221521961476747)
XLA Ops:
  0.0 1.0 convert_element_type.74
  1.0 1.0 slice.32
  2.1 3.4 %copy.51 = bf16[3,16,512,8]{1,3,2,0:T(8,128)(2,1)} copy(bf16[3,16,512,8]{2,3,1,0:T(8,128)(2,1)S(1)} %maximum_bitcast_fusion) | data formatting | bytes 786432 | tf_op jit(solution)/shard_map/transpose | solution.py:62
  5.5 2.9 %fusion.33 = (bf16[3,16,256]{1,2,0:T(8,128)(2,1)S(1)}, bf16[1,3,16,256]{2,3,1,0:T(8,128)(2,1)S(1)}, bf16[1,3,16,256]{2,3,1,0:T(8,128)(2,1)S(1)}, bf16[1,3,16,256...) fusion(bf16[3,16,4096]{1,2,0:T(8,128)(2,1)} %bitcast.172), kind=kLoop, calls=%fused_computation.84 | loop fusion | bytes 786432 | tf_op jit(solution)/shard_map/split | solution.py:66
  8.4 1.0 copy.53
  9.4 0.6 constant_dynamic-update-slice_fusion.15
  10.1 1.0 copy.54
  11.1 0.7 copy.55
  11.9 0.1 copy.57
  12.0 0.1 copy.58
  13.4 0.6 constant_dynamic-update-slice_fusion.14
  14.0 1.3 constant_dynamic-update-slice_fusion.13
  15.3 0.6 constant_dynamic-update-slice_fusion.12
  15.9 0.6 constant_dynamic-update-slice_fusion.11
  16.6 0.6 constant_dynamic-update-slice_fusion.10
  17.2 0.6 constant_dynamic-update-slice_fusion.9
  17.8 0.6 constant_dynamic-update-slice_fusion.8
  18.4 0.6 constant_dynamic-update-slice_fusion.7
  19.0 0.6 constant_dynamic-update-slice_fusion.6
  19.6 0.6 constant_dynamic-update-slice_fusion.5
  20.2 0.6 constant_dynamic-update-slice_fusion.4
  20.8 0.6 constant_dynamic-update-slice_fusion.3
  21.4 0.6 constant_dynamic-update-slice_fusion.2
  22.0 0.6 constant_dynamic-update-slice_fusion.1
  22.6 0.6 constant_dynamic-update-slice_fusion
  23.2 33.8 %all_to_all.56 = bf16[16,3,16,256]{3,2,1,0:T(8,128)(2,1)S(1)} all-to-all(bf16[16,3,16,256]{3,2,1,0:T(8,128)(2,1)} %constant_dynamic-update-slice_fusion), channel_id=1, replica_groups=mesh['row'=16,'col'=32] {'row'}, dimensions={0} | all-to-all | bytes 786432 | tf_op jit(solution)/shard_map/all_to_all | solution.py:66
  57.1 1.0 copy.71
  58.1 5.9 %all-to-all-start.2 = ((bf16[2,256,256]{2,0,1:T(2,128)(2,1)}), bf16[2,256,256]{2,0,1:T(2,128)(2,1)S(1)}, u32[]{:S(2)}, u32[]{:S(2)}) async-start(bf16[2,256,256]{2,0,1:T(2,128)(2,1)} %copy.71), calls=%async_computation.2 | async-start | bytes 524288 | tf_op jit(solution)/shard_map/all_to_all | solution.py:73
  64.1 2.5 %reshape.135 = bf16[32,8,32,8]{3,2,1,0:T(8,128)(2,1)S(1)} reshape(bf16[256,256]{1,0:T(8,128)(2,1)S(1)} %copy-done.7) | data formatting | bytes 262144 | tf_op jit(solution)/shard_map/reshape | solution.py:26
  66.5 1.9 copy.76
  68.4 2.5 %reshape.136 = bf16[32,8,32,8]{3,2,1,0:T(8,128)(2,1)S(1)} reshape(bf16[256,256]{1,0:T(8,128)(2,1)S(1)} %copy-done.8) | data formatting | bytes 262144 | tf_op jit(solution)/shard_map/reshape | solution.py:26
  70.9 1.9 copy.82
  72.8 0.1 copy.69
  72.9 0.4 all-to-all-done.2
  73.4 0.4 copy.73
  73.8 1.0 copy.74
  74.8 1.1 copy.78
  75.9 2.0 %fusion.1 = f32[1,8,32,32,8]{2,3,4,1,0:T(8,128)S(1)} fusion(bf16[32,8,32,8]{2,0,3,1:T(8,128)(2,1)} %copy.82, bf16[8,32,32,8,1]{1,3,2,0,4:T(8,128)(2,1)} %bitcast.186), kind=kOutput, calls=%fused_computation.2 | convolution fusion | flops 33619968 | bytes 524288 | tf_op jit(solution)/shard_map/sajxz,JZjz->saJxZ/dot_general | solution.py:27
  77.9 0.8 fusion.5
  78.7 0.7 fusion.4
  79.5 4.4 %copy.104 = f32[1,8,32,32,8]{1,4,3,2,0:T(8,128)} copy(f32[1,8,32,32,8]{2,3,4,1,0:T(8,128)S(1)} %fusion.4) | data formatting | bytes 524288 | tf_op jit(solution)/shard_map/reshape | solution.py:81
  83.8 0.5 broadcast.21
  84.4 38.4 %reduce = f32[8192,8]{1,0:T(8,128)} reduce(f32[8192,1,8]{2,1,0:T(1,128)} %bitcast.170, f32[]{:T(128)} %broadcast.21), dimensions={1}, to_apply=%bitcast.160.reduce_sub_computation | reduce | bytes 524292
  122.7 4.5 %reshape.152 = f32[32,1,2048]{2,1,0:T(1,128)} reshape(f32[8192,8]{1,0:T(8,128)} %reduce) | data formatting | bytes 524288
  127.3 7.3 %all-to-all-start.3 = ((f32[32,1,2048]{2,1,0:T(1,128)}), f32[32,1,2048]{2,1,0:T(1,128)S(1)}, u32[]{:S(2)}, u32[]{:S(2)}) async-start(f32[32,1,2048]{2,1,0:T(1,128)} %reshape.152), calls=%async_computation.3 | async-start | bytes 524288 | tf_op jit(solution)/shard_map/all_to_all | solution.py:82
  134.6 0.2 fusion.14
  134.9 0.2 fusion.13
  135.1 0.2 fusion.8
  135.4 0.8 copy.70
  136.2 7.7 %all-to-all-done.3 = f32[32,1,2048]{2,1,0:T(1,128)S(1)} async-done(((f32[32,1,2048]{2,1,0:T(1,128)}), f32[32,1,2048]{2,1,0:T(1,128)S(1)}, u32[]{:S(2)}, u32[]{:S(2)}) %all-to-all-start.3) | async-done | bytes 262176 | tf_op jit(solution)/shard_map/all_to_all | solution.py:82
  143.9 4.2 %all-to-all-start.1 = ((f32[1,256,256]{2,0,1:T(1,128)}), f32[1,256,256]{2,0,1:T(1,128)S(1)}, u32[]{:S(2)}, u32[]{:S(2)}) async-start(f32[1,256,256]{2,0,1:T(1,128)} %copy.70), calls=%async_computation.1 | async-start | bytes 524288 | tf_op jit(solution)/shard_map/all_to_all | solution.py:84
  148.1 1.2 reduce.1
  149.3 8.4 %reshape.153 = f32[8192,1,8]{2,1,0:T(1,128)} reshape(f32[32,2048]{1,0:T(8,128)S(1)} %reduce.1) | data formatting | bytes 524288
  157.7 2.9 %copy.105 = f32[1,8,32,256]{3,2,1,0:T(8,128)S(1)} copy(f32[1,8,32,256]{1,3,2,0:T(8,128)} %bitcast.171) | data formatting | bytes 524288 | tf_op jit(solution)/shard_map/all_to_all | solution.py:82
  160.6 0.2 copy.120
  160.8 1.0 copy.87
  161.7 3.0 %all-to-all-done.1 = f32[1,256,256]{2,0,1:T(1,128)S(1)} async-done(((f32[1,256,256]{2,0,1:T(1,128)}), f32[1,256,256]{2,0,1:T(1,128)S(1)}, u32[]{:S(2)}, u32[]{:S(2)}) %all-to-all-start.1) | async-done | bytes 262176 | tf_op jit(solution)/shard_map/all_to_all | solution.py:84
  164.7 9.1 %all-to-all-start.4 = ((f32[1,256,256]{2,0,1:T(1,128)}), f32[1,256,256]{2,0,1:T(1,128)S(1)}, u32[]{:S(2)}, u32[]{:S(2)}) async-start(f32[1,256,256]{2,0,1:T(1,128)} %copy.87), calls=%async_computation.4 | async-start | bytes 524288 | tf_op jit(solution)/shard_map/all_to_all | solution.py:85
  173.8 0.3 convolution_multiply_fusion.2
  174.1 0.3 fusion.9
  174.4 15.7 %all-to-all-done.4 = f32[1,256,256]{2,0,1:T(1,128)S(1)} async-done(((f32[1,256,256]{2,0,1:T(1,128)}), f32[1,256,256]{2,0,1:T(1,128)S(1)}, u32[]{:S(2)}, u32[]{:S(2)}) %all-to-all-start.4) | async-done | bytes 262176 | tf_op jit(solution)/shard_map/all_to_all | solution.py:85
  190.2 0.6 copy.90
  190.8 0.8 copy.91
  191.6 2.1 %fusion.17 = f32[1,16,8,512]{3,2,1,0:T(8,128)} fusion(f32[1,16,8,512]{3,2,1,0:T(8,128)S(1)} %copy-done.1, f32[16,8,512]{2,1,0:T(8,128)S(1)} %fusion.9, bf16[512,512]{1,0:T(8,128)(2,1)} %param.11, f32[1,16,512,8]{2,3,1,0:T(8,128)S(1)} %copy.91, bf16[1,16,8,512]{3,2,1,0:T(8,128)(2,1)S(1)} %convert_element_type.74), kind=kOutput, calls=%fused_computation.26 | convolution fusion | flops 67436544 | bytes 1703936 | tf_op jit(solution)/shard_map/dot_general | solution.py:11
  (40 shorter events, 1.6 us)
Async XLA Ops:
  0.0 173.8 %copy-start = (bf16[512,512]{1,0:T(8,128)(2,1)S(1)}, bf16[512,512]{1,0:T(8,128)(2,1)}, u32[]{:S(2)}) copy-start(bf16[512,512]{1,0:T(8,128)(2,1)} %param.10) | copy-start | bytes 1572868
  12.5 51.5 %copy-start.7 = (bf16[256,256]{1,0:T(8,128)(2,1)S(1)}, bf16[256,256]{1,0:T(8,128)(2,1)}, u32[]{:S(2)}) copy-start(bf16[256,256]{1,0:T(8,128)(2,1)} %param.14) | copy-start | bytes 393220
  57.1 11.3 %copy-start.8 = (bf16[256,256]{1,0:T(8,128)(2,1)S(1)}, bf16[256,256]{1,0:T(8,128)(2,1)}, u32[]{:S(2)}) copy-start(bf16[256,256]{1,0:T(8,128)(2,1)} %param.15) | copy-start | bytes 393220
  58.1 15.2 %all-to-all-start.2 = ((bf16[2,256,256]{2,0,1:T(2,128)(2,1)}), bf16[2,256,256]{2,0,1:T(2,128)(2,1)S(1)}, u32[]{:S(2)}, u32[]{:S(2)}) async-start(bf16[2,256,256]{2,0,1:T(2,128)(2,1)} %copy.71), calls=%async_computation.2 | async-start | bytes 524288 | tf_op jit(solution)/shard_map/all_to_all | solution.py:73
  73.4 4.5 %copy-start.3 = (bf16[32,8,32,8]{2,0,3,1:T(8,128)(2,1)S(1)}, bf16[32,8,32,8]{2,0,3,1:T(8,128)(2,1)}, u32[]{:S(2)}) copy-start(bf16[32,8,32,8]{2,0,3,1:T(8,128)(2,1)} %copy.76) | copy-start | bytes 393220
  75.9 2.0 %copy-start.5 = (bf16[1,8,32,256]{2,3,1,0:T(8,128)(2,1)S(1)}, bf16[1,8,32,256]{2,3,1,0:T(8,128)(2,1)}, u32[]{:S(2)}) copy-start(bf16[1,8,32,256]{2,3,1,0:T(8,128)(2,1)} %copy.74) | copy-start | bytes 393220
  75.9 2.8 %copy-start.4 = (bf16[1,8,32,256]{2,3,1,0:T(8,128)(2,1)S(1)}, bf16[1,8,32,256]{2,3,1,0:T(8,128)(2,1)}, u32[]{:S(2)}) copy-start(bf16[1,8,32,256]{2,3,1,0:T(8,128)(2,1)} %copy.78) | copy-start | bytes 393220
  122.7 11.9 %copy-start.6 = (bf16[256,256]{1,0:T(8,128)(2,1)S(1)}, bf16[256,256]{1,0:T(8,128)(2,1)}, u32[]{:S(2)}) copy-start(bf16[256,256]{1,0:T(8,128)(2,1)} %param.12) | copy-start | bytes 393220
  122.7 12.4 %copy-start.9 = (bf16[256,256]{1,0:T(8,128)(2,1)S(1)}, bf16[256,256]{1,0:T(8,128)(2,1)}, u32[]{:S(2)}) copy-start(bf16[256,256]{1,0:T(8,128)(2,1)} %param.13) | copy-start | bytes 393220
  127.3 16.6 %all-to-all-start.3 = ((f32[32,1,2048]{2,1,0:T(1,128)}), f32[32,1,2048]{2,1,0:T(1,128)S(1)}, u32[]{:S(2)}, u32[]{:S(2)}) async-start(f32[32,1,2048]{2,1,0:T(1,128)} %reshape.152), calls=%async_computation.3 | async-start | bytes 524288 | tf_op jit(solution)/shard_map/all_to_all | solution.py:82
  143.9 20.8 %all-to-all-start.1 = ((f32[1,256,256]{2,0,1:T(1,128)}), f32[1,256,256]{2,0,1:T(1,128)S(1)}, u32[]{:S(2)}, u32[]{:S(2)}) async-start(f32[1,256,256]{2,0,1:T(1,128)} %copy.70), calls=%async_computation.1 | async-start | bytes 524288 | tf_op jit(solution)/shard_map/all_to_all | solution.py:84
  157.7 16.1 %copy-start.2 = (bf16[3,16,8,512]{3,2,1,0:T(8,128)(2,1)S(1)}, bf16[3,16,8,512]{3,2,1,0:T(8,128)(2,1)}, u32[]{:S(2)}) copy-start(bf16[3,16,8,512]{3,2,1,0:T(8,128)(2,1)} %param.9) | copy-start | bytes 1179652
  164.7 25.5 %all-to-all-start.4 = ((f32[1,256,256]{2,0,1:T(1,128)}), f32[1,256,256]{2,0,1:T(1,128)S(1)}, u32[]{:S(2)}, u32[]{:S(2)}) async-start(f32[1,256,256]{2,0,1:T(1,128)} %copy.87), calls=%async_computation.4 | async-start | bytes 524288 | tf_op jit(solution)/shard_map/all_to_all | solution.py:85
  174.1 17.5 %copy-start.1 = (f32[1,16,8,512]{3,2,1,0:T(8,128)S(1)}, f32[1,16,8,512]{3,2,1,0:T(8,128)}, u32[]{:S(2)}) copy-start(f32[1,16,8,512]{3,2,1,0:T(8,128)} %param.8) | copy-start | bytes 786436
